TPU v7x, 32 devices: a whole 2x2x4 slice. The times are simulated.
32 devices in a mesh: dp: 8 (over z, x), tensor: 4 (over y, core).
Axes of the slice: x: 2, y: 2, z: 4, core: 2. Of those that a mesh axis runs over, the one named last changes fastest.
Arguments:
- inputs: bfloat16 [1500, 8, 1024], P('tensor', 'dp'), may hold values from -6 to 6
- segments: int32 [8, 1500], P('dp'), may hold values from 0 to 3, never falling along the last dimension, each value on 1 to 750 neighbouring positions
- cotangent: bfloat16 [1500, 8, 1024], P('tensor', 'dp'), may hold values from -6 to 6
- gain_one: float32 [1024], replicated, may hold values from 0.1 to 1.9
- first_in: bfloat16 [1024, 4096], P(None, 'tensor'), may hold values from -0.1875 to 0.1875
- first_out: bfloat16 [4096, 1024], P('tensor'), may hold values from -0.1875 to 0.1875
- gain_two: float32 [1024], replicated, may hold values from 0.1 to 1.9
- w_query: bfloat16 [1024, 1024], P(None, 'tensor'), may hold values from -0.1875 to 0.1875
- w_key: bfloat16 [1024, 1024], P(None, 'tensor'), may hold values from -0.1875 to 0.1875
- w_value: bfloat16 [1024, 1024], P(None, 'tensor'), may hold values from -0.1875 to 0.1875
- w_output: bfloat16 [1024, 1024], P('tensor'), may hold values from -0.75 to 0.75
- rel_table: float32 [16, 257], P('tensor'), may hold values from -4 to 4
- gain_three: float32 [1024], replicated, may hold values from 0.1 to 1.9
- w_glu: bfloat16 [1024, 2, 1024], P(None, None, 'tensor'), may hold values from -0.1875 to 0.1875
- kernel: float32 [31, 1024], P(None, 'tensor'), may hold values from -1 to 1
- w_back: bfloat16 [1024, 1024], P('tensor'), may hold values from -0.5 to 0.5
- gain_four: float32 [1024], replicated, may hold values from 0.1 to 1.9
- second_in: bfloat16 [1024, 4096], P(None, 'tensor'), may hold values from -0.1875 to 0.1875
- second_out: bfloat16 [4096, 1024], P('tensor'), may hold values from -0.1875 to 0.1875
- gain_five: float32 [1024], replicated, may hold values from 0.1 to 1.9
Outputs:
- output: bfloat16 [1500, 8, 1024], P('tensor', 'dp')
- grad_inputs: float32 [1500, 8, 1024], P('tensor', 'dp')
- grad_gain_one: float32 [1024], replicated
- grad_first_in: float32 [1024, 4096], P('dp', 'tensor')
- grad_first_out: float32 [4096, 1024], P('tensor', 'dp')
- grad_gain_two: float32 [1024], replicated
- grad_w_query: float32 [1024, 1024], P('dp', 'tensor')
- grad_w_key: float32 [1024, 1024], P('dp', 'tensor')
- grad_w_value: float32 [1024, 1024], P('dp', 'tensor')
- grad_w_output: float32 [1024, 1024], P('tensor', 'dp')
- grad_rel_table: float32 [16, 257], P('tensor')
- grad_gain_three: float32 [1024], replicated
- grad_w_glu: float32 [1024, 2, 1024], P('dp', None, 'tensor')
- grad_kernel: float32 [31, 1024], P(None, 'tensor')
- grad_w_back: float32 [1024, 1024], P('tensor', 'dp')
- grad_gain_four: float32 [1024], replicated
- grad_second_in: float32 [1024, 4096], P('dp', 'tensor')
- grad_second_out: float32 [4096, 1024], P('tensor', 'dp')
- grad_gain_five: float32 [1024], replicated
Inputs may be any that keep to these rules, and one draw needn't show every extreme that they name: `segments`: within each row of 1500 frames the segment numbers start at 0 and never fall; each of the 4 utterances holds 1 to 750 frames, and one holds exactly 750.
All inputs are finite; a program needn't handle non-finite values.
Results may differ from a plain program's by a relative error of at most 0.03.
Values may be sent and summed in bfloat16 or wider, within the bound.
No kernel may reach another device: no remote copies, remote signals or barrier semaphores. Data moves between devices by JAX's collectives and lax.ppermute only.
A program may use at most 256 MiB of HBM per device.

v0:
```python
import jax
import jax.numpy as jnp
from jax import lax
from jax.sharding import PartitionSpec as P

masked_score = -1e30


def normed(residual, gain_vec):
    row_mean = jnp.mean(residual, axis=-1, keepdims=True)
    centred = residual - row_mean
    variance = jnp.mean(centred * centred, axis=-1, keepdims=True)
    return centred * lax.rsqrt(variance + 1e-05) * gain_vec


def depthwise(values, kernel, labels):
    kernel_len = kernel.shape[0]
    half_width = kernel_len // 2
    frames = values.shape[0]
    padded = jnp.pad(values, ((half_width, half_width),) + ((0, 0),) * (values.ndim - 1))
    padded_labels = jnp.pad(
        labels, ((half_width, half_width),) + ((0, 0),) * (labels.ndim - 1), constant_values=-1
    )
    summed = jnp.zeros_like(values)
    for offset in range(kernel_len):
        same_seg = (padded_labels[offset : offset + frames] == labels)[..., None]
        summed = summed + jnp.where(
            same_seg, padded[offset : offset + frames] * kernel[offset], 0.0
        )
    return summed


def rel_band(table_row, frames):
    reach_max = table_row.shape[0] // 2
    distance = jnp.arange(2 * frames, dtype=jnp.int32) - (frames - 1)
    column = jnp.clip(distance, -reach_max, reach_max) + reach_max
    onehot = (column[None, :] == jnp.arange(table_row.shape[0], dtype=jnp.int32)[:, None]).astype(
        jnp.float32
    )
    diagonal_vals = jnp.dot(
        table_row, onehot, precision=lax.Precision.HIGHEST, preferred_element_type=jnp.float32
    )
    tiled = jnp.tile(diagonal_vals, frames)[: frames * (2 * frames - 1)]
    return tiled.reshape(frames, 2 * frames - 1)[:, frames - 1 :]


def gated_conv(glu_input, kernel, labels):
    channels = kernel.shape[1]
    gated = glu_input[..., :channels] * jax.nn.sigmoid(glu_input[..., channels:])
    return jax.nn.silu(depthwise(gated, kernel, labels))


def share_frames(local_rows):
    return lax.all_gather(local_rows, "tensor", axis=0, tiled=True)


def share_grads(local_rows):
    return lax.all_gather(local_rows, "tensor", axis=0, tiled=True)


def products(operands, transposed):
    summed = 0.0
    for operand, weight in operands:
        if transposed:
            summed = summed + jnp.einsum(
                "src,dc->srd", operand, weight, preferred_element_type=jnp.float32
            )
        else:
            summed = summed + jnp.einsum(
                "src,cd->srd", operand, weight, preferred_element_type=jnp.float32
            )
    return summed


def forward_sum(operands):
    return lax.psum_scatter(
        products(operands, False).astype(jnp.bfloat16), "tensor", scatter_dimension=0, tiled=True
    ).astype(jnp.float32)


def backward_sum(operands):
    return lax.psum_scatter(
        products(operands, True).astype(jnp.bfloat16), "tensor", scatter_dimension=0, tiled=True
    ).astype(jnp.float32)


def settle(grad_in, grad_out):
    return (
        lax.psum_scatter(grad_in, "dp", scatter_dimension=0, tiled=True),
        lax.psum_scatter(grad_out, "dp", scatter_dimension=1, tiled=True),
    )


def per_head(array, row_count, head_count):
    frames = array.shape[0]
    head_width = array.shape[2] // head_count
    return (
        array.reshape(frames, row_count, head_count, head_width)
        .transpose(1, 2, 0, 3)
        .reshape(row_count * head_count, frames, head_width)
    )


def per_frame(array, row_count, head_count):
    entries, frames, head_width = array.shape
    return (
        array.reshape(row_count, head_count, frames, head_width)
        .transpose(2, 0, 1, 3)
        .reshape(frames, row_count, head_count * head_width)
    )


def head_scores(query_head, key_head, rel_bias, label_row):
    score_scale = query_head.shape[-1] ** (-0.5)
    raw_scores = (
        jnp.einsum("qd,kd->qk", query_head, key_head, preferred_element_type=jnp.float32)
        * score_scale
        + rel_bias
    )
    allowed = label_row[:, None] == label_row[None, :]
    return jnp.where(allowed, raw_scores, masked_score)


def feed_forward(residual, gain_vec, w_in, w_out):
    local_rows = normed(residual, gain_vec).astype(jnp.bfloat16)
    gathered = share_frames(local_rows)
    hidden = jnp.einsum("srd,df->srf", gathered, w_in, preferred_element_type=jnp.float32)
    active = jax.nn.silu(hidden).astype(jnp.bfloat16)
    branch = forward_sum(((active, w_out),))
    return (residual + 0.5 * branch, (gathered, hidden, active))


def feed_back(incoming, residual, gain_vec, w_in, w_out, state):
    stored, hidden, active = state
    grad_branch = share_grads((0.5 * incoming).astype(jnp.bfloat16))
    grad_w_out = jnp.einsum("srf,srd->fd", active, grad_branch, preferred_element_type=jnp.float32)
    grad_active = jnp.einsum("srd,fd->srf", grad_branch, w_out, preferred_element_type=jnp.float32)
    sigmoid_vals = jax.nn.sigmoid(hidden)
    grad_hidden = (grad_active * sigmoid_vals * (1.0 + hidden * (1.0 - sigmoid_vals))).astype(
        jnp.bfloat16
    )
    grad_w_in = jnp.einsum("srd,srf->df", stored, grad_hidden, preferred_element_type=jnp.float32)
    grad_normed = backward_sum(((grad_hidden, w_in),))
    norm_value, norm_pull = jax.vjp(normed, residual, gain_vec)
    grad_residual, grad_gain = norm_pull(grad_normed)
    return (incoming + grad_residual, grad_gain, grad_w_in, grad_w_out)


def attention(residual, gain_vec, w_query, w_key, w_value, w_output, rel_table, segments):
    local_rows = normed(residual, gain_vec).astype(jnp.bfloat16)
    gathered = share_frames(local_rows)
    frames, row_count = (gathered.shape[0], gathered.shape[1])
    head_count = rel_table.shape[0]

    def project(weight):
        projected = jnp.einsum("srd,dc->src", gathered, weight, preferred_element_type=jnp.float32)
        return per_head(projected.astype(jnp.bfloat16), row_count, head_count)

    query_rows, key_rows, value_rows = (project(w_query), project(w_key), project(w_value))
    tables = jnp.tile(rel_table, (row_count, 1))
    labels = jnp.repeat(segments, head_count, axis=0)

    def one_head(record):
        query_head, key_head, value_head, table_row, label_row = record
        scores = head_scores(query_head, key_head, rel_band(table_row, frames), label_row)
        row_max = jnp.max(scores, axis=-1, keepdims=True)
        log_total = row_max + jnp.log(jnp.sum(jnp.exp(scores - row_max), axis=-1, keepdims=True))
        attend = jnp.exp(scores - log_total).astype(jnp.bfloat16)
        mixed = jnp.einsum("qk,kd->qd", attend, value_head, preferred_element_type=jnp.float32)
        return (mixed.astype(jnp.bfloat16), log_total[:, 0])

    attended, log_totals = lax.map(one_head, (query_rows, key_rows, value_rows, tables, labels))
    attended = per_frame(attended, row_count, head_count)
    branch = forward_sum(((attended, w_output),))
    return (residual + branch, (gathered, query_rows, key_rows, value_rows, attended, log_totals))


def attention_back(
    incoming, residual, gain_vec, w_query, w_key, w_value, w_output, rel_table, segments, state
):
    stored, query_rows, key_rows, value_rows, attended, log_totals = state
    frames, row_count = (stored.shape[0], stored.shape[1])
    head_count = rel_table.shape[0]
    grad_branch = share_grads(incoming.astype(jnp.bfloat16))
    grad_w_output = jnp.einsum(
        "src,srd->cd", attended, grad_branch, preferred_element_type=jnp.float32
    )
    grad_mixed = jnp.einsum(
        "srd,cd->src", grad_branch, w_output, preferred_element_type=jnp.float32
    )
    grad_mixed = per_head(grad_mixed.astype(jnp.bfloat16), row_count, head_count)
    tables = jnp.tile(rel_table, (row_count, 1))
    labels = jnp.repeat(segments, head_count, axis=0)

    def one_head(record):
        query_head, key_head, value_head, table_row, label_row, log_total, grad_head = record
        score_scale = query_head.shape[-1] ** (-0.5)
        rel_bias, band_pull = jax.vjp(lambda table_vals: rel_band(table_vals, frames), table_row)
        scores = head_scores(query_head, key_head, rel_bias, label_row)
        attend = jnp.exp(scores - log_total[:, None])
        grad_value = jnp.einsum(
            "qk,qd->kd", attend.astype(jnp.bfloat16), grad_head, preferred_element_type=jnp.float32
        )
        grad_attend = jnp.einsum(
            "qd,kd->qk", grad_head, value_head, preferred_element_type=jnp.float32
        )
        grad_scores = attend * (grad_attend - jnp.sum(attend * grad_attend, axis=-1, keepdims=True))
        grad_scores = grad_scores.astype(jnp.bfloat16)
        grad_query = (
            jnp.einsum("qk,kd->qd", grad_scores, key_head, preferred_element_type=jnp.float32)
            * score_scale
        )
        grad_key = (
            jnp.einsum("qk,qd->kd", grad_scores, query_head, preferred_element_type=jnp.float32)
            * score_scale
        )
        grad_table = band_pull(grad_scores.astype(jnp.float32))[0]
        return (
            grad_query.astype(jnp.bfloat16),
            grad_key.astype(jnp.bfloat16),
            grad_value.astype(jnp.bfloat16),
            grad_table,
        )

    grad_queries, grad_keys, grad_values, grad_tables = lax.map(
        one_head, (query_rows, key_rows, value_rows, tables, labels, log_totals, grad_mixed)
    )
    grad_queries = per_frame(grad_queries, row_count, head_count)
    grad_keys = per_frame(grad_keys, row_count, head_count)
    grad_values = per_frame(grad_values, row_count, head_count)
    grad_table = jnp.sum(grad_tables.reshape(row_count, head_count, grad_tables.shape[-1]), axis=0)
    stacked = jnp.stack([grad_queries, grad_keys, grad_values], axis=2)
    grad_projections = jnp.einsum(
        "srd,srtc->dtc", stored, stacked, preferred_element_type=jnp.float32
    )
    grad_normed = backward_sum(
        ((grad_queries, w_query), (grad_keys, w_key), (grad_values, w_value))
    )
    norm_value, norm_pull = jax.vjp(normed, residual, gain_vec)
    grad_residual, grad_gain = norm_pull(grad_normed)
    return (incoming + grad_residual, grad_gain, grad_table, grad_projections, grad_w_output)


def convolution(residual, gain_vec, w_glu, kernel, w_back, labels):
    local_rows = normed(residual, gain_vec).astype(jnp.bfloat16)
    gathered = share_frames(local_rows)
    channels = kernel.shape[1]
    glu_input = jnp.einsum(
        "srd,dc->src",
        gathered,
        w_glu.reshape(w_glu.shape[0], 2 * channels),
        preferred_element_type=jnp.float32,
    )
    active = gated_conv(glu_input, kernel, labels).astype(jnp.bfloat16)
    branch = forward_sum(((active, w_back),))
    return (residual + branch, (gathered, glu_input))


def convolution_back(incoming, residual, gain_vec, w_glu, kernel, w_back, labels, state):
    stored, glu_input = state
    channels = kernel.shape[1]
    width = w_glu.shape[0]
    glu_matrix = w_glu.reshape(width, 2 * channels)
    grad_branch = share_grads(incoming.astype(jnp.bfloat16))
    conv_value, conv_pull = jax.vjp(
        lambda glu_vals, taps: gated_conv(glu_vals, taps, labels), glu_input, kernel
    )
    active = conv_value.astype(jnp.bfloat16)
    grad_w_back = jnp.einsum("src,srd->cd", active, grad_branch, preferred_element_type=jnp.float32)
    grad_active = jnp.einsum("srd,cd->src", grad_branch, w_back, preferred_element_type=jnp.float32)
    grad_glu_input, grad_kernel = conv_pull(grad_active)
    grad_glu_input = grad_glu_input.astype(jnp.bfloat16)
    grad_w_glu = jnp.einsum(
        "srd,src->dc", stored, grad_glu_input, preferred_element_type=jnp.float32
    ).reshape(width, 2, channels)
    grad_normed = backward_sum(((grad_glu_input, glu_matrix),))
    norm_value, norm_pull = jax.vjp(normed, residual, gain_vec)
    grad_residual, grad_gain = norm_pull(grad_normed)
    return (incoming + grad_residual, grad_gain, grad_kernel, grad_w_glu, grad_w_back)


def shards(
    inputs,
    segments,
    cotangent,
    gain_one,
    first_in,
    first_out,
    gain_two,
    w_query,
    w_key,
    w_value,
    w_output,
    rel_table,
    gain_three,
    w_glu,
    kernel,
    w_back,
    gain_four,
    second_in,
    second_out,
    gain_five,
):
    frame_labels = segments.T
    start_frames = inputs.astype(jnp.float32)
    after_one, state_one = feed_forward(start_frames, gain_one, first_in, first_out)
    after_two, state_two = attention(
        after_one, gain_two, w_query, w_key, w_value, w_output, rel_table, segments
    )
    after_three, state_three = convolution(
        after_two, gain_three, w_glu, kernel, w_back, frame_labels
    )
    after_four, state_four = feed_forward(after_three, gain_four, second_in, second_out)
    final_rows, final_pull = jax.vjp(normed, after_four, gain_five)
    output = final_rows.astype(jnp.bfloat16)
    incoming, grad_five = final_pull(cotangent.astype(jnp.float32))
    incoming, grad_four, grad_second_in, grad_second_out = feed_back(
        incoming, after_three, gain_four, second_in, second_out, state_four
    )
    grad_second_in, grad_second_out = settle(grad_second_in, grad_second_out)
    incoming, grad_three, grad_kernel, grad_w_glu, grad_w_back = convolution_back(
        incoming, after_two, gain_three, w_glu, kernel, w_back, frame_labels, state_three
    )
    grad_w_glu, grad_w_back = settle(grad_w_glu, grad_w_back)
    incoming, grad_two, grad_table, grad_projections, grad_w_output = attention_back(
        incoming,
        after_one,
        gain_two,
        w_query,
        w_key,
        w_value,
        w_output,
        rel_table,
        segments,
        state_two,
    )
    grad_projections, grad_w_output = settle(grad_projections, grad_w_output)
    incoming, grad_one, grad_first_in, grad_first_out = feed_back(
        incoming, start_frames, gain_one, first_in, first_out, state_one
    )
    grad_first_in, grad_first_out = settle(grad_first_in, grad_first_out)
    grad_table, grad_kernel = lax.psum((grad_table, grad_kernel), "dp")
    grad_one, grad_two, grad_three, grad_four, grad_five = lax.psum(
        (grad_one, grad_two, grad_three, grad_four, grad_five), ("dp", "tensor")
    )
    return (
        output,
        incoming,
        grad_one,
        grad_first_in,
        grad_first_out,
        grad_two,
        grad_projections[:, 0],
        grad_projections[:, 1],
        grad_projections[:, 2],
        grad_w_output,
        grad_table,
        grad_three,
        grad_w_glu,
        grad_kernel,
        grad_w_back,
        grad_four,
        grad_second_in,
        grad_second_out,
        grad_five,
    )


def solution(mesh):
    in_specs = (
        P("tensor", "dp", None),
        P("dp", None),
        P("tensor", "dp", None),
        P(),
        P(None, "tensor"),
        P("tensor", None),
        P(),
        P(None, "tensor"),
        P(None, "tensor"),
        P(None, "tensor"),
        P("tensor", None),
        P("tensor", None),
        P(),
        P(None, None, "tensor"),
        P(None, "tensor"),
        P("tensor", None),
        P(),
        P(None, "tensor"),
        P("tensor", None),
        P(),
    )
    out_specs = (
        P("tensor", "dp", None),
        P("tensor", "dp", None),
        P(),
        P("dp", "tensor"),
        P("tensor", "dp"),
        P(),
        P("dp", "tensor"),
        P("dp", "tensor"),
        P("dp", "tensor"),
        P("tensor", "dp"),
        P("tensor", None),
        P(),
        P("dp", None, "tensor"),
        P(None, "tensor"),
        P("tensor", "dp"),
        P(),
        P("dp", "tensor"),
        P("tensor", "dp"),
        P(),
    )
    return jax.shard_map(shards, mesh=mesh, in_specs=in_specs, out_specs=out_specs, check_vma=False)
```

profile of v0, /device:TPU:0, one launch (start us, length us, event | category | flops | bytes accessed | tf_op | source)
XLA Modules:
  0.0 2913.9 jit_solution(12028822160477935282)
XLA Ops:
  20.7 48.4 %all-gather.9.cloned.1.call-done = bf16[1500,1,1024]{2,1,0:T(2,128)(2,1)} async-done(((bf16[375,1,1024]{2,1,0:T(2,128)(2,1)}), bf16[1500,1,1024]{2,1,0:T(2,128)(2,1)}) %all-gather.9.cloned.1.call-update) | async-done | bytes 3072016 | tf_op jit(solution)/shard_map/all_gather | solution.py:54
  83.4 30.9 %fusion = bf16[376,1024]{1,0:T(8,128)(2,1)S(1)} fusion(bf16[1500,1,1024]{2,0,1:T(8,128)(2,1)} %fusion.77), kind=kCustom, calls=%all-reduce-scatter | all-reduce-scatter fusion | flops 1540097 | bytes 3842560
  141.4 48.1 %all-gather.11.cloned.1.call-done = bf16[1500,1,1024]{2,1,0:T(2,128)(2,1)} async-done(((bf16[375,1,1024]{2,1,0:T(2,128)(2,1)}), bf16[1500,1,1024]{2,1,0:T(2,128)(2,1)}) %all-gather.11.cloned.1.call-update) | async-done | bytes 3072016 | tf_op jit(solution)/shard_map/all_gather | solution.py:54
  213.3 417.3 %while.32 = (s32[]{:T(128)}, bf16[4,1500,64]{1,2,0:T(8,128)(2,1)S(1)}, f32[4,1500]{1,0:T(4,128)S(1)}, s32[4,1500]{1,0:T(4,128)S(1)}, bf16[4,1500,64]{2,1,0:T(8,1...) while((s32[]{:T(128)}, ...), condition=%wide.region_8.9_spmd, body=%wide.region_5.8_spmd.sunk | while | flops 606376448 | bytes 199957408 | solution.py:172
  239.6 20.0 tile.35
  259.6 14.1 slice.666
  273.7 27.0 reshape.1090
  339.7 20.0 tile.35
  359.8 14.1 slice.666
  373.8 27.0 reshape.1090
  439.9 20.0 tile.35
  459.9 14.1 slice.666
  474.0 27.0 reshape.1090
  540.0 20.0 tile.35
  560.0 14.1 slice.666
  574.1 27.0 reshape.1090
  635.3 30.8 %fusion.1 = bf16[376,1024]{1,0:T(8,128)(2,1)S(1)} fusion(bf16[1500,1,1024]{2,0,1:T(8,128)(2,1)} %fusion.74), kind=kCustom, calls=%all-reduce-scatter.1 | all-reduce-scatter fusion | flops 1540097 | bytes 3842560
  689.4 46.0 %all-gather.13.cloned.1.call-done = bf16[1500,1,1024]{2,1,0:T(2,128)(2,1)} async-done(((bf16[375,1,1024]{2,1,0:T(2,128)(2,1)}), bf16[1500,1,1024]{2,1,0:T(2,128)(2,1)}) %all-gather.13.cloned.1.call-update) | async-done | bytes 3072016 | tf_op jit(solution)/shard_map/all_gather | solution.py:54
  741.9 12.0 select_add_fusion
  757.6 31.5 %fusion.2 = bf16[376,1024]{1,0:T(8,128)(2,1)} fusion(bf16[1500,1,1024]{2,0,1:T(8,128)(2,1)} %fusion.75), kind=kCustom, calls=%all-reduce-scatter.2 | all-reduce-scatter fusion | flops 1540097 | bytes 3842560
  815.9 49.6 %all-gather.15.cloned.1.call-done = bf16[1500,1,1024]{2,1,0:T(2,128)(2,1)} async-done(((bf16[375,1,1024]{2,1,0:T(2,128)(2,1)}), bf16[1500,1,1024]{2,1,0:T(2,128)(2,1)}) %all-gather.15.cloned.1.call-update) | async-done | bytes 3072016 | tf_op jit(solution)/shard_map/all_gather | solution.py:54
  880.0 30.8 %fusion.3 = bf16[376,1024]{1,0:T(8,128)(2,1)S(1)} fusion(bf16[1500,1,1024]{2,0,1:T(8,128)(2,1)} %fusion.78), kind=kCustom, calls=%all-reduce-scatter.3 | all-reduce-scatter fusion | flops 1540097 | bytes 3842560
  945.4 49.6 %all-gather.17.cloned.1.call-done = bf16[1500,1,1024]{2,1,0:T(2,128)(2,1)} async-done(((bf16[375,1,1024]{2,1,0:T(2,128)(2,1)}), bf16[1500,1,1024]{2,1,0:T(2,128)(2,1)}) %all-gather.17.cloned.1.call-update) | async-done | bytes 3072016 | tf_op jit(solution)/shard_map/all_gather | solution.py:58
  1010.9 30.8 %fusion.4 = bf16[376,1024]{1,0:T(8,128)(2,1)S(1)} fusion(bf16[1500,1,1024]{2,0,1:T(8,128)(2,1)} %fusion.79), kind=kCustom, calls=%all-reduce-scatter.4 | all-reduce-scatter fusion | flops 1540097 | bytes 3842560
  1067.4 49.6 %all-gather.19.cloned.1.call-done = bf16[1500,1,1024]{2,1,0:T(2,128)(2,1)} async-done(((bf16[375,1,1024]{2,1,0:T(2,128)(2,1)}), bf16[1500,1,1024]{2,1,0:T(2,128)(2,1)}) %all-gather.19.cloned.1.call-update) | async-done | bytes 3072016 | tf_op jit(solution)/shard_map/all_gather | solution.py:58
  1117.0 15.2 multiply_reduce_fusion.12
  1132.2 15.3 multiply_reduce_fusion.16
  1164.2 11.7 pad_add_fusion
  1185.5 30.8 %fusion.5 = bf16[376,1024]{1,0:T(8,128)(2,1)S(1)} fusion(bf16[1500,1,1024]{2,0,1:T(8,128)(2,1)} %fusion.73), kind=kCustom, calls=%all-reduce-scatter.5 | all-reduce-scatter fusion | flops 1540097 | bytes 3842560
  1242.2 49.6 %all-gather.21.cloned.1.call-done = bf16[1500,1,1024]{2,1,0:T(2,128)(2,1)} async-done(((bf16[375,1,1024]{2,1,0:T(2,128)(2,1)}), bf16[1500,1,1024]{2,1,0:T(2,128)(2,1)}) %all-gather.21.cloned.1.call-update) | async-done | bytes 3072016 | tf_op jit(solution)/shard_map/all_gather | solution.py:58
  1298.9 841.6 %while.33 = (s32[]{:T(128)}, bf16[4,1500,64]{1,2,0:T(8,128)(2,1)}, bf16[4,1500,64]{1,2,0:T(8,128)(2,1)}, bf16[4,1500,64]{1,2,0:T(8,128)(2,1)}, f32[4,257]{1,0:T(...) while((s32[]{:T(128)}, bf16[4,1500,64]{1,2,0:T(8,128)(2,1)}, ...), condition=%wide.region_29.30_spmd, body=%wide.region_26.29_spmd.sunk | while | flops 1494280448 | bytes 381868960 | solution.py:225
  1314.9 20.0 tile.37
  1335.0 14.0 slice.668
  1349.0 27.7 reshape.1092
  1444.2 23.3 reshape.1093
  1478.8 20.2 reshape.1094
  1523.7 20.0 tile.37
  1543.7 14.0 slice.668
  1557.8 27.7 reshape.1092
  1653.0 23.1 reshape.1093
  1676.2 11.2 pad_convert_fusion.2
  1687.4 20.2 reshape.1094
  1732.5 20.0 tile.37
  1752.5 14.0 slice.668
  1766.5 27.6 reshape.1092
  1861.7 23.1 reshape.1093
  1884.9 11.2 pad_convert_fusion.2
  1896.1 20.2 reshape.1094
  1941.2 20.0 tile.37
  1961.2 14.0 slice.668
  1975.3 27.6 reshape.1092
  2070.4 23.1 reshape.1093
  2104.8 20.2 reshape.1094
  2147.9 30.8 %fusion.6 = bf16[376,1024]{1,0:T(8,128)(2,1)S(1)} fusion(bf16[1500,1,1024]{2,0,1:T(8,128)(2,1)} %fusion.76), kind=kCustom, calls=%all-reduce-scatter.6 | all-reduce-scatter fusion | flops 1540097 | bytes 3842560
  2295.8 14.9 multiply_reduce_fusion.22
  2321.6 33.9 %fusion.7 = bf16[376,1024]{1,0:T(8,128)(2,1)S(1)} fusion(bf16[1500,1,1024]{2,0,1:T(8,128)(2,1)} %fusion.80), kind=kCustom, calls=%all-reduce-scatter.7 | all-reduce-scatter fusion | flops 1540097 | bytes 3842560
  2359.0 38.5 %all-reduce.85 = (f32[4,257]{1,0:T(4,128)}, f32[31,256]{1,0:T(8,128)}) all-reduce(f32[4,257]{1,0:T(4,128)S(1)} %get-tuple-element.278, f32[31,256]{1,0:T(8,128)S(1)} %pad_add_fusion.7), channel_id=1, replica_groups=mesh['dp'=8,'tensor'=4] {'dp'}, use_global_device_ids=true, to_apply=%region_44.45 | all-reduce | flops 8964 | bytes 71712 | tf_op jit(solution)/shard_map/psum | solution.py:342
  2410.1 39.0 %all-reduce.84 = (f32[1024]{0:T(1024)}, f32[1024]{0:T(1024)}, f32[1024]{0:T(1024)}, f32[1024]{0:T(1024)}, f32[1024]{0:T(1024)}) all-reduce(f32[1024]{0:T(1024)S(1)} %get-tuple-element.454, f32[1024]{0:T(1024)S(1)} %get-tuple-element.452, f32[1024]{0:T(1024)S(1)} %copy-done.103, ...), channel_id=1, replica_groups=mesh['dp'=8,'tensor'=4] {'dp','tensor'}, use_global_device_ids=true, to_apply=%region_37.38 | all-reduce | flops 5120 | bytes 40960 | tf_op jit(solution)/shard_map/psum | solution.py:343
  2460.0 11.7 reduce-scatter.43.cloned.1.call-done
  2471.6 91.5 %reduce-scatter.45.cloned.1.call-done = f32[128,1024]{1,0:T(8,128)} async-done(((f32[1024,1024]{1,0:T(8,128)}), f32[128,1024]{1,0:T(8,128)}) %reduce-scatter.45.cloned.1.call-update) | async-done | bytes 524304 | tf_op jit(solution)/shard_map/reduce_scatter | solution.py:89
  2563.1 92.5 %reduce-scatter.47.cloned.1.call-done = f32[1024,128]{1,0:T(8,128)} async-done(((f32[1024,1024]{1,0:T(8,128)}), f32[1024,128]{1,0:T(8,128)}) %reduce-scatter.47.cloned.1.call-update) | async-done | bytes 524304 | tf_op jit(solution)/shard_map/reduce_scatter | solution.py:90
  2655.6 67.8 %reduce-scatter.39.cloned.1.call-done = f32[256,128]{1,0:T(8,128)} async-done(((f32[256,1024]{1,0:T(8,128)}), f32[256,128]{1,0:T(8,128)}) %reduce-scatter.39.cloned.1.call-update) | async-done | bytes 131088 | tf_op jit(solution)/shard_map/reduce_scatter | solution.py:90
  2723.4 91.0 %reduce-scatter.33.cloned.1.call-done = f32[128,1024]{1,0:T(8,128)} async-done(((f32[1024,1024]{1,0:T(8,128)}), f32[128,1024]{1,0:T(8,128)}) %reduce-scatter.33.cloned.1.call-update) | async-done | bytes 524304 | tf_op jit(solution)/shard_map/reduce_scatter | solution.py:89
  2814.4 92.8 %reduce-scatter.35.cloned.1.call-done = f32[1024,128]{1,0:T(8,128)} async-done(((f32[1024,1024]{1,0:T(8,128)}), f32[1024,128]{1,0:T(8,128)}) %reduce-scatter.35.cloned.1.call-update) | async-done | bytes 524304 | tf_op jit(solution)/shard_map/reduce_scatter | solution.py:90
  (579 shorter events, 999.8 us)
Async XLA Ops:
  7.2 868.1 %copy-start = (bf16[1024,1024]{1,0:T(8,128)(2,1)S(1)}, bf16[1024,1024]{1,0:T(8,128)(2,1)}, u32[]{:S(2)}) copy-start(bf16[1024,1024]{1,0:T(8,128)(2,1)} %param.42) | copy-start | bytes 6291460
  7.2 61.8 %all-gather.9.cloned.1.call-start = ((), (), s32[]{:S(2)}) async-start(), calls=%async_computation.8 | async-start | bytes 7680000 | tf_op jit(solution)/shard_map/all_gather | solution.py:54
  20.6 168.9 %all-gather.11.cloned.1.call-start = ((), (), s32[]{:S(2)}) async-start(), calls=%async_computation.9 | async-start | bytes 7680000 | tf_op jit(solution)/shard_map/all_gather | solution.py:54
  83.4 32.7 %copy-start.118 = (u32[32]{0:T(128)S(1)}, u32[32]{0:T(128)}, u32[]{:S(2)}) copy-start(u32[32]{0:T(128)} %constant.348) | copy-start | bytes 388
  114.4 2.9 collective-permute-start
  140.7 594.7 %all-gather.13.cloned.1.call-start = ((), (), s32[]{:S(2)}) async-start(), calls=%async_computation.10 | async-start | bytes 7680000 | tf_op jit(solution)/shard_map/all_gather | solution.py:54
  141.4 53.7 %copy-start.42 = (bf16[1024,256]{1,0:T(8,128)(2,1)S(1)}, bf16[1024,256]{1,0:T(8,128)(2,1)}, u32[]{:S(2)}) copy-start(bf16[1024,256]{1,0:T(8,128)(2,1)} %param.32) | copy-start | bytes 1572868
  666.1 2.1 collective-permute-start.1
  685.8 179.7 %all-gather.15.cloned.1.call-start = ((), (), s32[]{:S(2)}) async-start(), calls=%async_computation.11 | async-start | bytes 7680000 | tf_op jit(solution)/shard_map/all_gather | solution.py:54
  688.5 459.1 %copy-start.86 = (pred[1500]{0:T(1024)(128)(4,1)}, pred[1500]{0:T(1024)(128)(4,1)S(1)}, u32[]{:S(2)}) copy-start(pred[1500]{0:T(1024)(128)(4,1)S(1)} %get-tuple-element.483) | copy-start | bytes 4504
  688.5 463.0 %copy-start.60 = (pred[1500]{0:T(1024)(128)(4,1)}, pred[1500]{0:T(1024)(128)(4,1)S(1)}, u32[]{:S(2)}) copy-start(pred[1500]{0:T(1024)(128)(4,1)S(1)} %get-tuple-element.484) | copy-start | bytes 4504
  688.5 468.8 %copy-start.62 = (pred[1500]{0:T(1024)(128)(4,1)}, pred[1500]{0:T(1024)(128)(4,1)S(1)}, u32[]{:S(2)}) copy-start(pred[1500]{0:T(1024)(128)(4,1)S(1)} %get-tuple-element.485) | copy-start | bytes 4504
  688.7 462.7 %copy-start.74 = (pred[1500]{0:T(1024)(128)(4,1)}, pred[1500]{0:T(1024)(128)(4,1)S(1)}, u32[]{:S(2)}) copy-start(pred[1500]{0:T(1024)(128)(4,1)S(1)} %get-tuple-element.471) | copy-start | bytes 4504
  688.8 462.7 %copy-start.76 = (pred[1500]{0:T(1024)(128)(4,1)}, pred[1500]{0:T(1024)(128)(4,1)S(1)}, u32[]{:S(2)}) copy-start(pred[1500]{0:T(1024)(128)(4,1)S(1)} %get-tuple-element.472) | copy-start | bytes 4504
  688.8 462.7 %copy-start.78 = (pred[1500]{0:T(1024)(128)(4,1)}, pred[1500]{0:T(1024)(128)(4,1)S(1)}, u32[]{:S(2)}) copy-start(pred[1500]{0:T(1024)(128)(4,1)S(1)} %get-tuple-element.473) | copy-start | bytes 4504
  688.8 468.5 %copy-start.68 = (pred[1500]{0:T(1024)(128)(4,1)}, pred[1500]{0:T(1024)(128)(4,1)S(1)}, u32[]{:S(2)}) copy-start(pred[1500]{0:T(1024)(128)(4,1)S(1)} %get-tuple-element.468) | copy-start | bytes 4504
  688.8 468.5 %copy-start.70 = (pred[1500]{0:T(1024)(128)(4,1)}, pred[1500]{0:T(1024)(128)(4,1)S(1)}, u32[]{:S(2)}) copy-start(pred[1500]{0:T(1024)(128)(4,1)S(1)} %get-tuple-element.469) | copy-start | bytes 4504
  688.8 468.5 %copy-start.72 = (pred[1500]{0:T(1024)(128)(4,1)}, pred[1500]{0:T(1024)(128)(4,1)S(1)}, u32[]{:S(2)}) copy-start(pred[1500]{0:T(1024)(128)(4,1)S(1)} %get-tuple-element.470) | copy-start | bytes 4504
  689.0 458.5 %copy-start.88 = (pred[1500]{0:T(1024)(128)(4,1)}, pred[1500]{0:T(1024)(128)(4,1)S(1)}, u32[]{:S(2)}) copy-start(pred[1500]{0:T(1024)(128)(4,1)S(1)} %get-tuple-element.479) | copy-start | bytes 4504
  689.1 458.5 %copy-start.90 = (pred[1500]{0:T(1024)(128)(4,1)}, pred[1500]{0:T(1024)(128)(4,1)S(1)}, u32[]{:S(2)}) copy-start(pred[1500]{0:T(1024)(128)(4,1)S(1)} %get-tuple-element.480) | copy-start | bytes 4504
  689.1 458.5 %copy-start.92 = (pred[1500]{0:T(1024)(128)(4,1)}, pred[1500]{0:T(1024)(128)(4,1)S(1)}, u32[]{:S(2)}) copy-start(pred[1500]{0:T(1024)(128)(4,1)S(1)} %get-tuple-element.481) | copy-start | bytes 4504
  689.1 458.5 %copy-start.94 = (pred[1500]{0:T(1024)(128)(4,1)}, pred[1500]{0:T(1024)(128)(4,1)S(1)}, u32[]{:S(2)}) copy-start(pred[1500]{0:T(1024)(128)(4,1)S(1)} %get-tuple-element.482) | copy-start | bytes 4504
  689.1 462.4 %copy-start.64 = (pred[1500]{0:T(1024)(128)(4,1)}, pred[1500]{0:T(1024)(128)(4,1)S(1)}, u32[]{:S(2)}) copy-start(pred[1500]{0:T(1024)(128)(4,1)S(1)} %get-tuple-element.477) | copy-start | bytes 4504
  689.1 462.4 %copy-start.66 = (pred[1500]{0:T(1024)(128)(4,1)}, pred[1500]{0:T(1024)(128)(4,1)S(1)}, u32[]{:S(2)}) copy-start(pred[1500]{0:T(1024)(128)(4,1)S(1)} %get-tuple-element.478) | copy-start | bytes 4504
  689.1 462.4 %copy-start.80 = (pred[1500]{0:T(1024)(128)(4,1)}, pred[1500]{0:T(1024)(128)(4,1)S(1)}, u32[]{:S(2)}) copy-start(pred[1500]{0:T(1024)(128)(4,1)S(1)} %get-tuple-element.474) | copy-start | bytes 4504
  689.1 462.4 %copy-start.82 = (pred[1500]{0:T(1024)(128)(4,1)}, pred[1500]{0:T(1024)(128)(4,1)S(1)}, u32[]{:S(2)}) copy-start(pred[1500]{0:T(1024)(128)(4,1)S(1)} %get-tuple-element.475) | copy-start | bytes 4504
  689.1 462.4 %copy-start.84 = (pred[1500]{0:T(1024)(128)(4,1)}, pred[1500]{0:T(1024)(128)(4,1)S(1)}, u32[]{:S(2)}) copy-start(pred[1500]{0:T(1024)(128)(4,1)S(1)} %get-tuple-element.476) | copy-start | bytes 4504
  789.9 2.1 collective-permute-start.2
  815.9 179.2 %all-gather.17.cloned.1.call-start = ((), (), s32[]{:S(2)}) async-start(), calls=%async_computation.12 | async-start | bytes 7680000 | tf_op jit(solution)/shard_map/all_gather | solution.py:58
  910.9 2.1 collective-permute-start.3
  945.4 171.6 %all-gather.19.cloned.1.call-start = ((), (), s32[]{:S(2)}) async-start(), calls=%async_computation.13 | async-start | bytes 7680000 | tf_op jit(solution)/shard_map/all_gather | solution.py:58
  1041.8 2.2 collective-permute-start.4
  1067.3 49.7 %copy-start.123 = (bf16[256,1024]{1,0:T(8,128)(2,1)S(1)}, bf16[256,1024]{1,0:T(8,128)(2,1)}, u32[]{:S(2)}) copy-start(bf16[256,1024]{1,0:T(8,128)(2,1)} %param.39) | copy-start | bytes 1572868
  1067.4 224.4 %all-gather.21.cloned.1.call-start = ((), (), s32[]{:S(2)}) async-start(), calls=%async_computation.14 | async-start | bytes 7680000 | tf_op jit(solution)/shard_map/all_gather | solution.py:58
  1132.2 25.1 copy-start.3
  1216.4 2.2 collective-permute-start.5
  1242.2 49.7 %copy-start.124 = (bf16[256,1024]{1,0:T(8,128)(2,1)S(1)}, bf16[256,1024]{1,0:T(8,128)(2,1)}, u32[]{:S(2)}) copy-start(bf16[256,1024]{1,0:T(8,128)(2,1)} %param.34) | copy-start | bytes 1572868
  1242.2 1020.0 %all-gather.23.cloned.1.call-start = ((), (), s32[]{:S(2)}) async-start(), calls=%async_computation.15 | async-start | bytes 7680000 | tf_op jit(solution)/shard_map/all_gather | solution.py:58
  1298.9 841.6 %copy-start.43 = (bf16[1024,256]{1,0:T(8,128)(2,1)S(1)}, bf16[1024,256]{1,0:T(8,128)(2,1)}, u32[]{:S(2)}) copy-start(bf16[1024,256]{1,0:T(8,128)(2,1)} %param.32) | copy-start | bytes 1572868
  2179.6 2.2 collective-permute-start.6
  2205.8 151.3 %reduce-scatter.41.cloned.1.call-start = ((), (), s32[]{:S(2)}) async-start(), calls=%async_computation.20 | async-start | bytes 2359296 | tf_op jit(solution)/shard_map/reduce_scatter | solution.py:89
  2219.8 238.4 %reduce-scatter.37.cloned.1.call-start = ((), (), s32[]{:S(2)}) async-start(), calls=%async_computation.18 | async-start | bytes 3538944 | tf_op jit(solution)/shard_map/reduce_scatter | solution.py:89
  2229.2 242.4 %reduce-scatter.43.cloned.1.call-start = ((), (), s32[]{:S(2)}) async-start(), calls=%async_computation.21 | async-start | bytes 1179648 | tf_op jit(solution)/shard_map/reduce_scatter | solution.py:90
  2235.9 327.3 %reduce-scatter.45.cloned.1.call-start = ((), (), s32[]{:S(2)}) async-start(), calls=%async_computation.22 | async-start | bytes 4718592 | tf_op jit(solution)/shard_map/reduce_scatter | solution.py:89
  2245.6 410.0 %reduce-scatter.47.cloned.1.call-start = ((), (), s32[]{:S(2)}) async-start(), calls=%async_computation.23 | async-start | bytes 4718592 | tf_op jit(solution)/shard_map/reduce_scatter | solution.py:90
  2256.1 467.3 %reduce-scatter.39.cloned.1.call-start = ((), (), s32[]{:S(2)}) async-start(), calls=%async_computation.19 | async-start | bytes 1179648 | tf_op jit(solution)/shard_map/reduce_scatter | solution.py:90
  2262.1 552.3 %reduce-scatter.33.cloned.1.call-start = ((), (), s32[]{:S(2)}) async-start(), calls=%async_computation.16 | async-start | bytes 4718592 | tf_op jit(solution)/shard_map/reduce_scatter | solution.py:89
  2282.0 625.2 %reduce-scatter.35.cloned.1.call-start = ((), (), s32[]{:S(2)}) async-start(), calls=%async_computation.17 | async-start | bytes 4718592 | tf_op jit(solution)/shard_map/reduce_scatter | solution.py:90
  2321.5 35.3 %copy-start.105 = (f32[256]{0:T(256)S(1)}, f32[256]{0:T(256)}, u32[]{:S(2)}) copy-start(f32[256]{0:T(256)} %get-tuple-element.433) | copy-start | bytes 3076
  2321.5 35.3 %copy-start.106 = (f32[256]{0:T(256)S(1)}, f32[256]{0:T(256)}, u32[]{:S(2)}) copy-start(f32[256]{0:T(256)} %get-tuple-element.434) | copy-start | bytes 3076
  2321.5 35.3 %copy-start.107 = (f32[256]{0:T(256)S(1)}, f32[256]{0:T(256)}, u32[]{:S(2)}) copy-start(f32[256]{0:T(256)} %get-tuple-element.435) | copy-start | bytes 3076
  2321.5 35.4 %copy-start.108 = (f32[256]{0:T(256)S(1)}, f32[256]{0:T(256)}, u32[]{:S(2)}) copy-start(f32[256]{0:T(256)} %get-tuple-element.436) | copy-start | bytes 3076
  2321.5 35.4 %copy-start.109 = (f32[256]{0:T(256)S(1)}, f32[256]{0:T(256)}, u32[]{:S(2)}) copy-start(f32[256]{0:T(256)} %get-tuple-element.437) | copy-start | bytes 3076
  2321.5 35.4 %copy-start.110 = (f32[256]{0:T(256)S(1)}, f32[256]{0:T(256)}, u32[]{:S(2)}) copy-start(f32[256]{0:T(256)} %get-tuple-element.438) | copy-start | bytes 3076
  2321.6 35.4 %copy-start.111 = (f32[256]{0:T(256)S(1)}, f32[256]{0:T(256)}, u32[]{:S(2)}) copy-start(f32[256]{0:T(256)} %get-tuple-element.439) | copy-start | bytes 3076
  2321.6 35.4 %copy-start.112 = (f32[256]{0:T(256)S(1)}, f32[256]{0:T(256)}, u32[]{:S(2)}) copy-start(f32[256]{0:T(256)} %get-tuple-element.440) | copy-start | bytes 3076
  2321.6 35.4 %copy-start.113 = (f32[256]{0:T(256)S(1)}, f32[256]{0:T(256)}, u32[]{:S(2)}) copy-start(f32[256]{0:T(256)} %get-tuple-element.441) | copy-start | bytes 3076
  2321.6 35.4 %copy-start.114 = (f32[256]{0:T(256)S(1)}, f32[256]{0:T(256)}, u32[]{:S(2)}) copy-start(f32[256]{0:T(256)} %get-tuple-element.442) | copy-start | bytes 3076
  2321.6 35.4 %copy-start.115 = (f32[256]{0:T(256)S(1)}, f32[256]{0:T(256)}, u32[]{:S(2)}) copy-start(f32[256]{0:T(256)} %get-tuple-element.443) | copy-start | bytes 3076
  2321.6 35.4 %copy-start.116 = (f32[256]{0:T(256)S(1)}, f32[256]{0:T(256)}, u32[]{:S(2)}) copy-start(f32[256]{0:T(256)} %get-tuple-element.444) | copy-start | bytes 3076
  2321.6 35.4 %copy-start.117 = (f32[256]{0:T(256)S(1)}, f32[256]{0:T(256)}, u32[]{:S(2)}) copy-start(f32[256]{0:T(256)} %get-tuple-element.445) | copy-start | bytes 3076
  2355.6 41.9 %collective-permute-start.7 = (bf16[3,1024]{1,0:T(4,128)(2,1)S(1)}, bf16[3,1024]{1,0:T(4,128)(2,1)S(1)}, u32[]{:S(2)}, u32[]{:S(2)}) collective-permute-start(bf16[3,1024]{1,0:T(4,128)(2,1)S(1)} %slice.522), channel_id=1, source_target_pairs={{0,1},{1,2},{2,3},{4,5},{5,6},{6,7},{8,9},{9,10},{10,11},{12,13},{... | collective-permute-start | bytes 18440
  2403.8 45.3 %copy-start.98 = (f32[375]{0:T(512)S(1)}, f32[375]{0:T(512)}, u32[]{:S(2)}) copy-start(f32[375]{0:T(512)} %copy-done.97) | copy-start | bytes 4504
  2455.3 451.9 %copy-start.1 = (bf16[1024,1024]{1,0:T(8,128)(2,1)S(1)}, bf16[1024,1024]{1,0:T(8,128)(2,1)}, u32[]{:S(2)}) copy-start(bf16[1024,1024]{1,0:T(8,128)(2,1)} %param.42) | copy-start | bytes 6291460
  (93 other events, 503.2 us)
Sparse Core Ops, SparseCore 0:
  20.7 48.2 all-gather.8
  140.9 48.6 all-gather.10
  686.0 49.4 all-gather.12
  816.0 49.4 all-gather.14
  945.5 49.4 all-gather.16
  1067.5 49.4 all-gather.18
  1242.3 49.4 all-gather.20
  2205.9 49.4 all-gather.22
  2258.9 67.8 reduce-scatter.40
  2330.3 74.2 reduce-scatter.36
  2408.6 62.9 reduce-scatter.42
  2476.1 86.9 reduce-scatter.44
  2567.3 88.2 reduce-scatter.46
  2659.8 63.5 reduce-scatter.38
  2727.5 86.9 reduce-scatter.32
  2818.9 88.2 reduce-scatter.34
where the time goes:
time: 2930 us; the launch traced here: 2910 us
  local copies, waits for them, and re-layouts  1070 us (37%)
  waiting for transfers between devices  793 us (27%)
  other arithmetic  347 us (12%)
  blocking collectives  328 us (11%)
  matrix products  324 us (11%)
    reshape x12, local copies, waits for them, and re-layouts, rel_band(): return tiled.reshape(frames, 2 * frames - 1)[:, frames - 1:]  311 us
    reduce_scatter x4, waiting for transfers between devices, settle(): lax.psum_scatter(grad_out, 'dp', scatter_dimension=1, tiled=True)  265 us
    unnamed x8, blocking collectives  250 us
    another operation x16, local copies, waits for them, and re-layouts, rel_band(): tiled = jnp.tile(diagonal_vals, frames)[:frames * (2 * frames - 1)]  229 us
    all_gather x4, waiting for transfers between devices, share_frames(): return lax.all_gather(local_rows, 'tensor', axis=0, tiled=True)  192 us
    reduce_scatter x4, waiting for transfers between devices, settle(): lax.psum_scatter(grad_in, 'dp', scatter_dimension=0, tiled=True)  183 us
    all_gather x4, waiting for transfers between devices, share_grads(): return lax.all_gather(local_rows, 'tensor', axis=0, tiled=True)  149 us
    slice x8, local copies, waits for them, and re-layouts, rel_band(): tiled = jnp.tile(diagonal_vals, frames)[:frames * (2 * frames - 1)]  112 us
  transfers between devices with their start and end apart: 24, of which 19 were waited for; matrix products, arithmetic and copies ran while one was open for 6% of the time, Pallas kernels for 0%

commit v1 on v0

--- a/solution.py
+++ b/solution.py
@@ -1,9 +1,37 @@
+import functools
 import jax
 import jax.numpy as jnp
 from jax import lax
 from jax.sharding import PartitionSpec as P
 
 masked_score = -1e30
+
+
+def raise_rows_all(inp, where_dim):
+    work_now = list(inp.shape[1:])
+    work_now[where_dim] *= inp.shape[0]
+    local_now = jnp.moveaxis(inp, 0, where_dim).reshape(work_now)
+    return local_now
+
+
+def name_windows_by_axis(mine_x, ax_name, join_dim):
+    degree = lax.axis_size(ax_name)
+    views = tuple(((u, (u + 1) % degree) for u in range(degree)))
+    steps_seen = tuple(((pp, nth) for nth, pp in views))
+    after, t1 = ([], [])
+    for tick in tuple(range(degree - 1)):
+        if tick % 2 == 0:
+            after.append(lax.ppermute(after[-1] if after else mine_x, ax_name, perm=views))
+        else:
+            t1.append(lax.ppermute(t1[-1] if t1 else mine_x, ax_name, steps_seen))
+    d_next = jnp.stack([*after[::-1], mine_x, *t1])
+    small = lax.axis_index(ax_name) - len(after)
+    d_next = d_next[(jnp.arange(degree) - small) % degree]
+    reached = raise_rows_all(d_next, join_dim)
+    return reached
+
+
+quarters_advance = functools.partial(name_windows_by_axis, ax_name="tensor", join_dim=0)
 
 
 def normed(residual, gain_vec):
@@ -51,7 +79,7 @@
 
 
 def share_frames(local_rows):
-    return lax.all_gather(local_rows, "tensor", axis=0, tiled=True)
+    return quarters_advance(local_rows)
 
 
 def share_grads(local_rows):

time: 2930 us -> 2800 us (0.956)
  other arithmetic: 347 us -> 247 us
  waiting for transfers between devices: 793 us -> 696 us
  local copies, waits for them, and re-layouts: 1070 us -> 1100 us
    all_gather x4 -> x0, waiting for transfers between devices: 192 us -> none  [share_frames(): return lax.all_gather(local_rows, 'tensor', axis=0, tiled=True)]
    ppermute x0 -> x12, waiting for transfers between devices: none -> 83.4 us  [the longest x8 83.4 us: name_windows_by_axis(): lax.ppermute(after[-1] if after else mine_x, ax_name, perm=views)]
    reduce_sum x5 -> x2, other arithmetic: 31.6 us -> 2.21 us  [normed(): centred = residual - row_mean]
    unnamed x287 -> x300, local copies, waits for them, and re-layouts: 92.9 us -> 65.9 us
  transfers between devices with their start and end apart: 24 -> 32, of which waited for: 19 -> 23; matrix products, arithmetic and copies ran while one was open for 6% -> 6% of each run, Pallas kernels for 0% -> 0%
where the time goes in v1:
time: 2800 us; the launch traced here: 2780 us
  local copies, waits for them, and re-layouts  1100 us (39%)
  waiting for transfers between devices  696 us (25%)
  blocking collectives  344 us (12%)
  matrix products  314 us (11%)
  other arithmetic  247 us (9%)
  starting transfers between devices  39.6 us (1%)
    reshape x12, local copies, waits for them, and re-layouts, rel_band(): return tiled.reshape(frames, 2 * frames - 1)[:, frames - 1:]  311 us
    reduce_scatter x4, waiting for transfers between devices, settle(): lax.psum_scatter(grad_out, 'dp', scatter_dimension=1, tiled=True)  275 us
    unnamed x8, blocking collectives  266 us
    another operation x16, local copies, waits for them, and re-layouts, rel_band(): tiled = jnp.tile(diagonal_vals, frames)[:frames * (2 * frames - 1)]  229 us
    reduce_scatter x4, waiting for transfers between devices, settle(): lax.psum_scatter(grad_in, 'dp', scatter_dimension=0, tiled=True)  184 us
    all_gather x4, waiting for transfers between devices, share_grads(): return lax.all_gather(local_rows, 'tensor', axis=0, tiled=True)  148 us
    slice x8, local copies, waits for them, and re-layouts, rel_band(): tiled = jnp.tile(diagonal_vals, frames)[:frames * (2 * frames - 1)]  112 us
    while x20, local copies, waits for them, and re-layouts  103 us
  transfers between devices with their start and end apart: 32, of which 23 were waited for; matrix products, arithmetic and copies ran while one was open for 6% of the time, Pallas kernels for 0%

profile of v1, /device:TPU:0, one launch (start us, length us, event | category | flops | bytes accessed | tf_op | source)
XLA Modules:
  0.0 2778.7 jit_solution(1136383429245849540)
XLA Ops:
  14.4 15.4 collective-permute-done
  66.6 34.7 %fusion = bf16[376,1024]{1,0:T(8,128)(2,1)} fusion(bf16[1500,1,1024]{2,0,1:T(8,128)(2,1)} %fusion.77), kind=kCustom, calls=%all-reduce-scatter | all-reduce-scatter fusion | flops 1540097 | bytes 3842560
  117.0 13.0 collective-permute-done.3
  174.7 417.1 %while.32 = (s32[]{:T(128)}, bf16[4,1500,64]{1,2,0:T(8,128)(2,1)S(1)}, f32[4,1500]{1,0:T(4,128)S(1)}, s32[4,1500]{1,0:T(4,128)S(1)}, bf16[4,1500,64]{2,1,0:T(8,1...) while((s32[]{:T(128)}, ...), condition=%wide.region_8.9_spmd, body=%wide.region_5.8_spmd.sunk | while | flops 606376448 | bytes 199957408 | solution.py:200
  200.8 20.0 tile.35
  220.8 14.0 slice.674
  234.9 27.0 reshape.1197
  300.9 20.0 tile.35
  320.9 14.0 slice.674
  335.0 27.0 reshape.1197
  401.0 20.0 tile.35
  421.0 14.0 slice.674
  435.1 27.0 reshape.1197
  501.1 20.0 tile.35
  521.2 14.0 slice.674
  535.2 27.0 reshape.1197
  595.8 35.8 %fusion.1 = bf16[376,1024]{1,0:T(8,128)(2,1)} fusion(bf16[1500,1,1024]{2,0,1:T(8,128)(2,1)} %fusion.74), kind=kCustom, calls=%all-reduce-scatter.1 | all-reduce-scatter fusion | flops 1540097 | bytes 3842560
  646.6 11.4 collective-permute-done.6
  687.4 11.9 select_add_fusion
  703.1 35.5 %fusion.2 = bf16[376,1024]{1,0:T(8,128)(2,1)S(1)} fusion(bf16[1500,1,1024]{2,0,1:T(8,128)(2,1)} %fusion.75), kind=kCustom, calls=%all-reduce-scatter.2 | all-reduce-scatter fusion | flops 1540097 | bytes 3842560
  750.9 13.2 collective-permute-done.9
  800.6 34.4 %fusion.3 = bf16[376,1024]{1,0:T(8,128)(2,1)S(1)} fusion(bf16[1500,1,1024]{2,0,1:T(8,128)(2,1)} %fusion.78), kind=kCustom, calls=%all-reduce-scatter.3 | all-reduce-scatter fusion | flops 1540097 | bytes 3842560
  851.6 49.1 %all-gather.5.cloned.1.call-done = bf16[1500,1,1024]{2,1,0:T(2,128)(2,1)} async-done(((bf16[375,1,1024]{2,1,0:T(2,128)(2,1)}), bf16[1500,1,1024]{2,1,0:T(2,128)(2,1)}) %all-gather.5.cloned.1.call-update) | async-done | bytes 3072016 | tf_op jit(solution)/shard_map/all_gather | solution.py:86
  916.3 30.8 %fusion.4 = bf16[376,1024]{1,0:T(8,128)(2,1)S(1)} fusion(bf16[1500,1,1024]{2,0,1:T(8,128)(2,1)} %fusion.79), kind=kCustom, calls=%all-reduce-scatter.4 | all-reduce-scatter fusion | flops 1540097 | bytes 3842560
  959.6 49.6 %all-gather.7.cloned.1.call-done = bf16[1500,1,1024]{2,1,0:T(2,128)(2,1)} async-done(((bf16[375,1,1024]{2,1,0:T(2,128)(2,1)}), bf16[1500,1,1024]{2,1,0:T(2,128)(2,1)}) %all-gather.7.cloned.1.call-update) | async-done | bytes 3072016 | tf_op jit(solution)/shard_map/all_gather | solution.py:86
  1009.2 15.1 multiply_reduce_fusion.12
  1024.3 15.2 multiply_reduce_fusion.16
  1056.2 11.7 pad_add_fusion
  1077.5 30.8 %fusion.5 = bf16[376,1024]{1,0:T(8,128)(2,1)S(1)} fusion(bf16[1500,1,1024]{2,0,1:T(8,128)(2,1)} %fusion.73), kind=kCustom, calls=%all-reduce-scatter.5 | all-reduce-scatter fusion | flops 1540097 | bytes 3842560
  1120.8 49.6 %all-gather.9.cloned.1.call-done = bf16[1500,1,1024]{2,1,0:T(2,128)(2,1)} async-done(((bf16[375,1,1024]{2,1,0:T(2,128)(2,1)}), bf16[1500,1,1024]{2,1,0:T(2,128)(2,1)}) %all-gather.9.cloned.1.call-update) | async-done | bytes 3072016 | tf_op jit(solution)/shard_map/all_gather | solution.py:86
  1177.4 840.8 %while.33 = (s32[]{:T(128)}, bf16[4,1500,64]{1,2,0:T(8,128)(2,1)}, bf16[4,1500,64]{1,2,0:T(8,128)(2,1)}, bf16[4,1500,64]{1,2,0:T(8,128)(2,1)}, f32[4,257]{1,0:T(...) while((s32[]{:T(128)}, bf16[4,1500,64]{1,2,0:T(8,128)(2,1)}, ...), condition=%wide.region_29.30_spmd, body=%wide.region_26.29_spmd.sunk | while | flops 1494280448 | bytes 381868960 | solution.py:253
  1193.3 20.1 tile.37
  1213.4 14.1 slice.676
  1227.5 27.7 reshape.1199
  1322.4 23.1 reshape.1200
  1345.6 11.2 pad_convert_fusion.2
  1356.7 20.2 reshape.1201
  1401.8 20.1 tile.37
  1421.9 14.1 slice.676
  1436.0 27.6 reshape.1199
  1530.8 23.1 reshape.1200
  1553.9 11.2 pad_convert_fusion.2
  1565.1 20.2 reshape.1201
  1610.2 20.1 tile.37
  1630.3 14.1 slice.676
  1644.3 27.6 reshape.1199
  1739.2 23.1 reshape.1200
  1773.5 20.2 reshape.1201
  1818.6 20.1 tile.37
  1838.7 14.1 slice.676
  1852.8 27.6 reshape.1199
  1947.6 23.1 reshape.1200
  1981.9 20.2 reshape.1201
  2025.5 30.8 %fusion.6 = bf16[376,1024]{1,0:T(8,128)(2,1)S(1)} fusion(bf16[1500,1,1024]{2,0,1:T(8,128)(2,1)} %fusion.76), kind=kCustom, calls=%all-reduce-scatter.6 | all-reduce-scatter fusion | flops 1540097 | bytes 3842560
  2162.1 14.5 multiply_reduce_fusion.22
  2187.6 33.7 %fusion.7 = bf16[376,1024]{1,0:T(8,128)(2,1)S(1)} fusion(bf16[1500,1,1024]{2,0,1:T(8,128)(2,1)} %fusion.80), kind=kCustom, calls=%all-reduce-scatter.7 | all-reduce-scatter fusion | flops 1540097 | bytes 3842560
  2224.7 38.8 %all-reduce.85 = (f32[4,257]{1,0:T(4,128)}, f32[31,256]{1,0:T(8,128)}) all-reduce(f32[4,257]{1,0:T(4,128)S(1)} %get-tuple-element.278, f32[31,256]{1,0:T(8,128)S(1)} %pad_add_fusion.7), channel_id=1, replica_groups=mesh['dp'=8,'tensor'=4] {'dp'}, use_global_device_ids=true, to_apply=%region_44.45 | all-reduce | flops 8964 | bytes 71712 | tf_op jit(solution)/shard_map/psum | solution.py:370
  2271.7 38.3 %all-reduce.84 = (f32[1024]{0:T(1024)}, f32[1024]{0:T(1024)}, f32[1024]{0:T(1024)}, f32[1024]{0:T(1024)}, f32[1024]{0:T(1024)}) all-reduce(f32[1024]{0:T(1024)S(1)} %get-tuple-element.454, f32[1024]{0:T(1024)S(1)} %get-tuple-element.446, f32[1024]{0:T(1024)S(1)} %copy-done.112, ...), channel_id=1, replica_groups=mesh['dp'=8,'tensor'=4] {'dp','tensor'}, use_global_device_ids=true, to_apply=%region_37.38 | all-reduce | flops 5120 | bytes 40960 | tf_op jit(solution)/shard_map/psum | solution.py:371
  2311.9 23.5 reduce-scatter.43.cloned.1.call-done
  2335.4 92.2 %reduce-scatter.47.cloned.1.call-done = f32[1024,128]{1,0:T(8,128)} async-done(((f32[1024,1024]{1,0:T(8,128)}), f32[1024,128]{1,0:T(8,128)}) %reduce-scatter.47.cloned.1.call-update) | async-done | bytes 524304 | tf_op jit(solution)/shard_map/reduce_scatter | solution.py:118
  2427.6 92.1 %reduce-scatter.45.cloned.1.call-done = f32[128,1024]{1,0:T(8,128)} async-done(((f32[1024,1024]{1,0:T(8,128)}), f32[128,1024]{1,0:T(8,128)}) %reduce-scatter.45.cloned.1.call-update) | async-done | bytes 524304 | tf_op jit(solution)/shard_map/reduce_scatter | solution.py:117
  2519.6 67.8 %reduce-scatter.39.cloned.1.call-done = f32[256,128]{1,0:T(8,128)} async-done(((f32[256,1024]{1,0:T(8,128)}), f32[256,128]{1,0:T(8,128)}) %reduce-scatter.39.cloned.1.call-update) | async-done | bytes 131088 | tf_op jit(solution)/shard_map/reduce_scatter | solution.py:118
  2587.5 91.7 %reduce-scatter.35.cloned.1.call-done = f32[1024,128]{1,0:T(8,128)} async-done(((f32[1024,1024]{1,0:T(8,128)}), f32[1024,128]{1,0:T(8,128)}) %reduce-scatter.35.cloned.1.call-update) | async-done | bytes 524304 | tf_op jit(solution)/shard_map/reduce_scatter | solution.py:118
  2679.2 92.2 %reduce-scatter.33.cloned.1.call-done = f32[128,1024]{1,0:T(8,128)} async-done(((f32[1024,1024]{1,0:T(8,128)}), f32[128,1024]{1,0:T(8,128)}) %reduce-scatter.33.cloned.1.call-update) | async-done | bytes 524304 | tf_op jit(solution)/shard_map/reduce_scatter | solution.py:117
  (627 shorter events, 975.6 us)
Async XLA Ops:
  7.2 788.7 %copy-start = (bf16[1024,1024]{1,0:T(8,128)(2,1)S(1)}, bf16[1024,1024]{1,0:T(8,128)(2,1)}, u32[]{:S(2)}) copy-start(bf16[1024,1024]{1,0:T(8,128)(2,1)} %param.42) | copy-start | bytes 6291460
  7.2 893.4 %all-gather.5.cloned.1.call-start = ((), (), s32[]{:S(2)}) async-start(), calls=%async_computation.8 | async-start | bytes 7680000 | tf_op jit(solution)/shard_map/all_gather | solution.py:86
  12.0 17.8 collective-permute-start
  12.5 20.3 collective-permute-start.2
  29.8 11.6 collective-permute-start.1
  32.4 113.5 %copy-start.114 = (s32[1024]{0:T(1024)}, s32[1024]{0:T(1024)S(1)}, u32[]{:S(2)}) copy-start(s32[1024]{0:T(1024)S(1)} %pad_clamp_fusion) | copy-start | bytes 12292
  66.6 36.7 %copy-start.128 = (u32[32]{0:T(128)S(1)}, u32[32]{0:T(128)}, u32[]{:S(2)}) copy-start(u32[32]{0:T(128)} %constant.380) | copy-start | bytes 388
  102.0 2.5 collective-permute-start.12
  114.7 15.3 collective-permute-start.3
  117.0 18.3 collective-permute-start.5
  130.1 12.7 collective-permute-start.4
  632.4 2.1 collective-permute-start.13
  643.4 14.5 collective-permute-start.6
  645.9 397.6 %copy-start.81 = (pred[1500]{0:T(1024)(128)(4,1)}, pred[1500]{0:T(1024)(128)(4,1)S(1)}, u32[]{:S(2)}) copy-start(pred[1500]{0:T(1024)(128)(4,1)S(1)} %get-tuple-element.471) | copy-start | bytes 4504
  645.9 397.6 %copy-start.83 = (pred[1500]{0:T(1024)(128)(4,1)}, pred[1500]{0:T(1024)(128)(4,1)S(1)}, u32[]{:S(2)}) copy-start(pred[1500]{0:T(1024)(128)(4,1)S(1)} %get-tuple-element.472) | copy-start | bytes 4504
  645.9 397.6 %copy-start.85 = (pred[1500]{0:T(1024)(128)(4,1)}, pred[1500]{0:T(1024)(128)(4,1)S(1)}, u32[]{:S(2)}) copy-start(pred[1500]{0:T(1024)(128)(4,1)S(1)} %get-tuple-element.473) | copy-start | bytes 4504
  646.0 403.4 %copy-start.75 = (pred[1500]{0:T(1024)(128)(4,1)}, pred[1500]{0:T(1024)(128)(4,1)S(1)}, u32[]{:S(2)}) copy-start(pred[1500]{0:T(1024)(128)(4,1)S(1)} %get-tuple-element.468) | copy-start | bytes 4504
  646.0 403.3 %copy-start.77 = (pred[1500]{0:T(1024)(128)(4,1)}, pred[1500]{0:T(1024)(128)(4,1)S(1)}, u32[]{:S(2)}) copy-start(pred[1500]{0:T(1024)(128)(4,1)S(1)} %get-tuple-element.469) | copy-start | bytes 4504
  646.0 403.3 %copy-start.79 = (pred[1500]{0:T(1024)(128)(4,1)}, pred[1500]{0:T(1024)(128)(4,1)S(1)}, u32[]{:S(2)}) copy-start(pred[1500]{0:T(1024)(128)(4,1)S(1)} %get-tuple-element.470) | copy-start | bytes 4504
  646.2 393.3 %copy-start.95 = (pred[1500]{0:T(1024)(128)(4,1)}, pred[1500]{0:T(1024)(128)(4,1)S(1)}, u32[]{:S(2)}) copy-start(pred[1500]{0:T(1024)(128)(4,1)S(1)} %get-tuple-element.479) | copy-start | bytes 4504
  646.2 393.3 %copy-start.97 = (pred[1500]{0:T(1024)(128)(4,1)}, pred[1500]{0:T(1024)(128)(4,1)S(1)}, u32[]{:S(2)}) copy-start(pred[1500]{0:T(1024)(128)(4,1)S(1)} %get-tuple-element.480) | copy-start | bytes 4504
  646.2 393.3 %copy-start.99 = (pred[1500]{0:T(1024)(128)(4,1)}, pred[1500]{0:T(1024)(128)(4,1)S(1)}, u32[]{:S(2)}) copy-start(pred[1500]{0:T(1024)(128)(4,1)S(1)} %get-tuple-element.481) | copy-start | bytes 4504
  646.3 393.3 %copy-start.101 = (pred[1500]{0:T(1024)(128)(4,1)}, pred[1500]{0:T(1024)(128)(4,1)S(1)}, u32[]{:S(2)}) copy-start(pred[1500]{0:T(1024)(128)(4,1)S(1)} %get-tuple-element.482) | copy-start | bytes 4504
  646.3 397.3 %copy-start.71 = (pred[1500]{0:T(1024)(128)(4,1)}, pred[1500]{0:T(1024)(128)(4,1)S(1)}, u32[]{:S(2)}) copy-start(pred[1500]{0:T(1024)(128)(4,1)S(1)} %get-tuple-element.477) | copy-start | bytes 4504
  646.3 397.3 %copy-start.73 = (pred[1500]{0:T(1024)(128)(4,1)}, pred[1500]{0:T(1024)(128)(4,1)S(1)}, u32[]{:S(2)}) copy-start(pred[1500]{0:T(1024)(128)(4,1)S(1)} %get-tuple-element.478) | copy-start | bytes 4504
  646.3 397.3 %copy-start.87 = (pred[1500]{0:T(1024)(128)(4,1)}, pred[1500]{0:T(1024)(128)(4,1)S(1)}, u32[]{:S(2)}) copy-start(pred[1500]{0:T(1024)(128)(4,1)S(1)} %get-tuple-element.474) | copy-start | bytes 4504
  646.3 397.3 %copy-start.89 = (pred[1500]{0:T(1024)(128)(4,1)}, pred[1500]{0:T(1024)(128)(4,1)S(1)}, u32[]{:S(2)}) copy-start(pred[1500]{0:T(1024)(128)(4,1)S(1)} %get-tuple-element.475) | copy-start | bytes 4504
  646.3 397.3 %copy-start.91 = (pred[1500]{0:T(1024)(128)(4,1)}, pred[1500]{0:T(1024)(128)(4,1)S(1)}, u32[]{:S(2)}) copy-start(pred[1500]{0:T(1024)(128)(4,1)S(1)} %get-tuple-element.476) | copy-start | bytes 4504
  646.6 18.5 collective-permute-start.8
  658.0 13.6 collective-permute-start.7
  664.5 375.1 %copy-start.93 = (pred[1500]{0:T(1024)(128)(4,1)}, pred[1500]{0:T(1024)(128)(4,1)S(1)}, u32[]{:S(2)}) copy-start(pred[1500]{0:T(1024)(128)(4,1)S(1)} %get-tuple-element.483) | copy-start | bytes 4504
  664.5 379.1 %copy-start.65 = (pred[1500]{0:T(1024)(128)(4,1)}, pred[1500]{0:T(1024)(128)(4,1)S(1)}, u32[]{:S(2)}) copy-start(pred[1500]{0:T(1024)(128)(4,1)S(1)} %get-tuple-element.484) | copy-start | bytes 4504
  664.5 384.8 %copy-start.67 = (pred[1500]{0:T(1024)(128)(4,1)}, pred[1500]{0:T(1024)(128)(4,1)S(1)}, u32[]{:S(2)}) copy-start(pred[1500]{0:T(1024)(128)(4,1)S(1)} %get-tuple-element.485) | copy-start | bytes 4504
  738.6 2.1 collective-permute-start.14
  748.6 15.6 collective-permute-start.9
  750.9 18.0 collective-permute-start.11
  764.2 12.6 collective-permute-start.10
  835.0 2.1 collective-permute-start.15
  851.5 157.7 %all-gather.7.cloned.1.call-start = ((), (), s32[]{:S(2)}) async-start(), calls=%async_computation.9 | async-start | bytes 7680000 | tf_op jit(solution)/shard_map/all_gather | solution.py:86
  947.2 2.2 collective-permute-start.16
  957.3 52.0 %copy-start.134 = (bf16[256,1024]{1,0:T(8,128)(2,1)S(1)}, bf16[256,1024]{1,0:T(8,128)(2,1)}, u32[]{:S(2)}) copy-start(bf16[256,1024]{1,0:T(8,128)(2,1)} %param.39) | copy-start | bytes 1572868
  959.6 210.8 %all-gather.9.cloned.1.call-start = ((), (), s32[]{:S(2)}) async-start(), calls=%async_computation.10 | async-start | bytes 7680000 | tf_op jit(solution)/shard_map/all_gather | solution.py:86
  1108.4 2.2 collective-permute-start.17
  1118.4 52.0 %copy-start.135 = (bf16[256,1024]{1,0:T(8,128)(2,1)S(1)}, bf16[256,1024]{1,0:T(8,128)(2,1)}, u32[]{:S(2)}) copy-start(bf16[256,1024]{1,0:T(8,128)(2,1)} %param.34) | copy-start | bytes 1572868
  1120.8 1012.0 %all-gather.11.cloned.1.call-start = ((), (), s32[]{:S(2)}) async-start(), calls=%async_computation.11 | async-start | bytes 7680000 | tf_op jit(solution)/shard_map/all_gather | solution.py:86
  1177.4 840.8 %copy-start.46 = (bf16[1024,256]{1,0:T(8,128)(2,1)S(1)}, bf16[1024,256]{1,0:T(8,128)(2,1)}, u32[]{:S(2)}) copy-start(bf16[1024,256]{1,0:T(8,128)(2,1)} %param.32) | copy-start | bytes 1572868
  2056.4 2.2 collective-permute-start.18
  2069.9 153.0 %reduce-scatter.41.cloned.1.call-start = ((), (), s32[]{:S(2)}) async-start(), calls=%async_computation.16 | async-start | bytes 2359296 | tf_op jit(solution)/shard_map/reduce_scatter | solution.py:117
  2086.2 223.9 %reduce-scatter.37.cloned.1.call-start = ((), (), s32[]{:S(2)}) async-start(), calls=%async_computation.14 | async-start | bytes 3538944 | tf_op jit(solution)/shard_map/reduce_scatter | solution.py:117
  2101.0 234.4 %reduce-scatter.43.cloned.1.call-start = ((), (), s32[]{:S(2)}) async-start(), calls=%async_computation.17 | async-start | bytes 1179648 | tf_op jit(solution)/shard_map/reduce_scatter | solution.py:118
  2107.6 320.0 %reduce-scatter.47.cloned.1.call-start = ((), (), s32[]{:S(2)}) async-start(), calls=%async_computation.19 | async-start | bytes 4718592 | tf_op jit(solution)/shard_map/reduce_scatter | solution.py:118
  2118.3 401.4 %reduce-scatter.45.cloned.1.call-start = ((), (), s32[]{:S(2)}) async-start(), calls=%async_computation.18 | async-start | bytes 4718592 | tf_op jit(solution)/shard_map/reduce_scatter | solution.py:117
  2126.6 460.9 %reduce-scatter.39.cloned.1.call-start = ((), (), s32[]{:S(2)}) async-start(), calls=%async_computation.15 | async-start | bytes 1179648 | tf_op jit(solution)/shard_map/reduce_scatter | solution.py:118
  2132.7 546.5 %reduce-scatter.35.cloned.1.call-start = ((), (), s32[]{:S(2)}) async-start(), calls=%async_computation.13 | async-start | bytes 4718592 | tf_op jit(solution)/shard_map/reduce_scatter | solution.py:118
  2143.1 628.3 %reduce-scatter.33.cloned.1.call-start = ((), (), s32[]{:S(2)}) async-start(), calls=%async_computation.12 | async-start | bytes 4718592 | tf_op jit(solution)/shard_map/reduce_scatter | solution.py:117
  2187.5 35.1 %copy-start.119 = (f32[256]{0:T(256)S(1)}, f32[256]{0:T(256)}, u32[]{:S(2)}) copy-start(f32[256]{0:T(256)} %get-tuple-element.437) | copy-start | bytes 3076
  2187.5 35.1 %copy-start.120 = (f32[256]{0:T(256)S(1)}, f32[256]{0:T(256)}, u32[]{:S(2)}) copy-start(f32[256]{0:T(256)} %get-tuple-element.438) | copy-start | bytes 3076
  2187.5 35.1 %copy-start.121 = (f32[256]{0:T(256)S(1)}, f32[256]{0:T(256)}, u32[]{:S(2)}) copy-start(f32[256]{0:T(256)} %get-tuple-element.439) | copy-start | bytes 3076
  2187.5 35.1 %copy-start.122 = (f32[256]{0:T(256)S(1)}, f32[256]{0:T(256)}, u32[]{:S(2)}) copy-start(f32[256]{0:T(256)} %get-tuple-element.440) | copy-start | bytes 3076
  2187.5 35.1 %copy-start.123 = (f32[256]{0:T(256)S(1)}, f32[256]{0:T(256)}, u32[]{:S(2)}) copy-start(f32[256]{0:T(256)} %get-tuple-element.441) | copy-start | bytes 3076
  2221.2 44.0 %copy-start.54 = (f32[1024]{0:T(1024)S(1)}, f32[1024]{0:T(1024)}, u32[]{:S(2)}) copy-start(f32[1024]{0:T(1024)} %param.27) | copy-start | bytes 12292
  2221.3 44.0 %copy-start.57 = (f32[375]{0:T(512)S(1)}, f32[375]{0:T(512)}, u32[]{:S(2)}) copy-start(f32[375]{0:T(512)} %copy-done.56) | copy-start | bytes 4504
  2221.3 42.3 %collective-permute-start.19 = (bf16[3,1024]{1,0:T(4,128)(2,1)S(1)}, bf16[3,1024]{1,0:T(4,128)(2,1)S(1)}, u32[]{:S(2)}, u32[]{:S(2)}) collective-permute-start(bf16[3,1024]{1,0:T(4,128)(2,1)S(1)} %slice.530), channel_id=1, source_target_pairs={{0,1},{1,2},{2,3},{4,5},{5,6},{6,7},{8,9},{9,10},{10,11},{12,13},{... | collective-permute-start | bytes 18440
  2267.0 504.4 %copy-start.1 = (bf16[1024,1024]{1,0:T(8,128)(2,1)S(1)}, bf16[1024,1024]{1,0:T(8,128)(2,1)}, u32[]{:S(2)}) copy-start(bf16[1024,1024]{1,0:T(8,128)(2,1)} %param.42) | copy-start | bytes 6291460
  (112 other events, 915.4 us)
Sparse Core Ops, SparseCore 0:
  851.6 48.9 all-gather.4
  959.7 49.4 all-gather.6
  1120.9 49.4 all-gather.8
  2070.0 49.4 all-gather.10
  2122.8 67.6 reduce-scatter.40
  2194.0 74.0 reduce-scatter.36
  2272.1 63.3 reduce-scatter.42
  2340.1 87.4 reduce-scatter.46
  2431.8 87.7 reduce-scatter.44
  2523.8 63.5 reduce-scatter.38
  2591.7 87.4 reduce-scatter.34
  2683.7 87.6 reduce-scatter.32
